TPU v7x, 32 devices: a whole 2x2x4 slice. The times are simulated.
32 devices in a mesh: grp: 8 (over z, y), rep: 2 (over core), tp: 2 (over x).
Axes of the slice: x: 2, y: 2, z: 4, core: 2. Of those that a mesh axis runs over, the one named last changes fastest.
Arguments:
- hidden: bfloat16 [8, 768, 8192], P('grp', 'rep'), may hold values from -6 to 6
- decode_hidden: bfloat16 [8, 2, 2, 32, 8192], P('grp', 'rep'), may hold values from -6 to 6
- norm_gain: bfloat16 [8192], replicated, may hold values from 0.25 to 1.75
- qkv_weight: bfloat16 [8192, 10240], P('grp', 'tp'), may hold values from -0.0625 to 0.0625
- qkv_bias: bfloat16 [10240], P('tp'), may hold values from -32 to 32
- lengths: int32 [8], replicated, may hold values from 12 to 768, as said below
Outputs:
- prefill_out: bfloat16 [8, 768, 8192], P('grp', 'rep', 'tp')
- decode_out: bfloat16 [8, 2, 2, 32, 8192], P('grp', 'rep', None, None, 'tp')
Inputs may be any that keep to these rules, and one draw needn't show every extreme that they name: `lengths`: some prompt is 768 tokens long.
All inputs are finite; a program needn't handle non-finite values.
Results may differ from a plain program's by a relative error of at most 0.012.
The roundings to bfloat16 on the way count: a program that leaves them out, or rounds other values in their place, can miss the bound.
Values may be sent and summed in bfloat16 or wider, within the bound.
A program may use at most 256 MiB of HBM per device.

v0:
```python
import jax
import jax.numpy as jnp
from jax import lax
from jax.sharding import PartitionSpec as P

HD = 128
QPK = 8
STEPS = 4
THETA = 1000000.0
EPSILON = 1e-06
NEGATIVE = -1e30


def shifted(block, axis, distance):
    devices = range(lax.axis_size(axis))
    route = [((i - distance) % len(devices), i) for i in devices]
    return lax.ppermute(block, axis, route)


def normalize(row_block, gain_row):
    widened = row_block.astype(jnp.float32)
    factor = lax.rsqrt(jnp.mean(widened * widened, axis=-1, keepdims=True) + EPSILON)
    return (widened * factor * gain_row.astype(jnp.float32)).astype(jnp.bfloat16)


def rope_tables(positions, head_size):
    half_size = head_size // 2
    frequency = THETA ** (-(jnp.arange(half_size, dtype=jnp.float32) * 2.0 / head_size))
    angle = positions.astype(jnp.float32)[:, None] * frequency[None, :]
    return (jnp.cos(angle), jnp.sin(angle))


def rotate(vector, cosine, sine_part):
    half_size = vector.shape[-1] // 2
    first_half = vector[..., :half_size]
    second = vector[..., half_size:]
    return jnp.concatenate(
        [first_half * cosine - second * sine_part, second * cosine + first_half * sine_part],
        axis=-1,
    )


def masked_max(scores, allowed):
    return jnp.max(jnp.where(allowed, scores, NEGATIVE), axis=-1, keepdims=True)


def combine_values(weight_matrix, value_matrix):
    return jnp.einsum(
        "aprk,kaz->rapz",
        weight_matrix.astype(jnp.bfloat16),
        value_matrix,
        preferred_element_type=jnp.float32,
    )


def pair_scores(query_matrix, key_matrix_rows, score_scale):
    return (
        jnp.einsum(
            "wjro,ujo->jrwu", query_matrix, key_matrix_rows, preferred_element_type=jnp.float32
        )
        * score_scale
    )


def decode_pair(
    query_matrix,
    own_keys,
    own_values,
    prompt_keys,
    prompt_values,
    valid_len,
    local_allowed,
    score_scale,
):
    key_slot_index = jnp.arange(prompt_keys.shape[0], dtype=jnp.int32)
    prompt_allowed = (key_slot_index < valid_len)[None, None, None, :]
    far_scores = pair_scores(query_matrix, prompt_keys, score_scale)
    near_scores = pair_scores(query_matrix, own_keys, score_scale)
    highest = jnp.maximum(
        masked_max(far_scores, prompt_allowed), masked_max(near_scores, local_allowed)
    )
    far_exp = jnp.where(prompt_allowed, jnp.exp(far_scores - highest), 0.0)
    near_exp = jnp.where(local_allowed, jnp.exp(near_scores - highest), 0.0)
    running = jnp.sum(far_exp, axis=-1, keepdims=True) + jnp.sum(near_exp, axis=-1, keepdims=True)
    return combine_values(far_exp / running, prompt_values) + combine_values(
        near_exp / running, own_values
    )


def on_device(hidden, decode_hidden, norm_gain, qkv_weight, qkv_bias, lengths):
    prompt_count = lax.axis_size("grp")
    rep_count = lax.axis_size("rep")
    half_cycle = prompt_count // 2
    grp_here = lax.axis_index("grp")
    rep_here = lax.axis_index("rep")
    span_rows = hidden.shape[1]
    model_width = hidden.shape[2]
    head_block = (QPK + 2) * HD
    heads_here = qkv_bias.shape[0] // head_block
    decode_rows = decode_hidden.shape[3]
    score_scale = HD ** (-0.5)
    prefill_normed = normalize(hidden[0], norm_gain)
    decode_normed = normalize(decode_hidden.reshape(2 * decode_rows, model_width), norm_gain)
    normed = jnp.concatenate([prefill_normed, decode_normed], axis=0)
    share_cols = qkv_weight.shape[1] // rep_count
    own_cols = lax.dynamic_slice_in_dim(qkv_weight, rep_here * share_cols, share_cols, 1)
    columns = lax.all_gather(own_cols, "grp", axis=0, tiled=True)
    complete = lax.all_gather(columns, "rep", axis=1, tiled=True)
    projected = jnp.dot(normed, complete, preferred_element_type=jnp.float32)
    projected = (projected + qkv_bias.astype(jnp.float32)).reshape(
        normed.shape[0], heads_here, QPK + 2, HD
    )
    index_table = jnp.arange(prompt_count, dtype=jnp.int32)

    def length_of(prompt):
        return jnp.sum(jnp.where(index_table == prompt, lengths, 0))

    own_len = length_of(grp_here)
    far_len = length_of((grp_here + half_cycle) % prompt_count)
    row_position = rep_here * span_rows + jnp.arange(span_rows, dtype=jnp.int32)
    local_ids = jnp.arange(decode_rows, dtype=jnp.int32)
    step_ids = local_ids % STEPS
    sample_ids = local_ids // STEPS
    positions = jnp.concatenate([row_position, own_len + step_ids, far_len + step_ids])
    cosine, sine_part = rope_tables(positions, HD)
    query_matrix = rotate(
        projected[:, :, :QPK], cosine[:, None, None, :], sine_part[:, None, None, :]
    ).astype(jnp.bfloat16)
    key_matrix_rows = rotate(
        projected[:, :, QPK], cosine[:, None, :], sine_part[:, None, :]
    ).astype(jnp.bfloat16)
    value_matrix = projected[:, :, QPK + 1].astype(jnp.bfloat16)
    cache_keys, cache_values = (
        lax.all_gather(key_matrix_rows[:span_rows], "rep", axis=0, tiled=True),
        lax.all_gather(value_matrix[:span_rows], "rep", axis=0, tiled=True),
    )
    key_pos = jnp.arange(cache_keys.shape[0], dtype=jnp.int32)
    allowed = ((key_pos[None, :] <= row_position[:, None]) & (key_pos[None, :] < own_len))[
        None, None
    ]
    scores = pair_scores(query_matrix[:span_rows], cache_keys, score_scale)
    highest = masked_max(scores, allowed)
    exponent = jnp.where(allowed, jnp.exp(scores - highest), 0.0)
    weight_matrix = exponent / jnp.sum(exponent, axis=-1, keepdims=True)
    attended = combine_values(weight_matrix, cache_values)
    prefill_out = attended.astype(jnp.bfloat16).reshape(1, span_rows, heads_here * QPK * HD)
    decode_queries = query_matrix[span_rows:].reshape(2, decode_rows, heads_here, QPK, HD)
    decode_keys = key_matrix_rows[span_rows:].reshape(2, decode_rows, heads_here, HD)
    decode_values = value_matrix[span_rows:].reshape(2, decode_rows, heads_here, HD)
    local_allowed = (
        (sample_ids[None, :] == sample_ids[:, None]) & (step_ids[None, :] <= step_ids[:, None])
    )[None, None]
    near_out = decode_pair(
        decode_queries[0],
        decode_keys[0],
        decode_values[0],
        cache_keys,
        cache_values,
        own_len,
        local_allowed,
        score_scale,
    )
    far_keys, far_values = shifted((cache_keys, cache_values), "grp", half_cycle)
    far_out = decode_pair(
        decode_queries[1],
        decode_keys[1],
        decode_values[1],
        far_keys,
        far_values,
        far_len,
        local_allowed,
        score_scale,
    )
    decode_out = (
        jnp.stack([near_out, far_out])
        .astype(jnp.bfloat16)
        .reshape(1, 1, 2, decode_rows, heads_here * QPK * HD)
    )
    return (prefill_out, decode_out)


def solution(mesh):
    return jax.shard_map(
        on_device,
        mesh=mesh,
        in_specs=(
            P("grp", "rep", None),
            P("grp", "rep", None, None, None),
            P(),
            P("grp", "tp"),
            P("tp"),
            P(),
        ),
        out_specs=(P("grp", "rep", "tp"), P("grp", "rep", None, None, "tp")),
        check_vma=False,
    )
```

profile of v0, /device:TPU:0, one launch (start us, length us, event | category | flops | bytes accessed | tf_op | source)
XLA Modules:
  0.0 1132.9 jit_solution(10912499802913706107)
XLA Ops:
  7.2 0.0 all-gather.4.cloned.1.call-start
  7.2 5.1 constant_dynamic-slice_fusion
  12.4 0.0 all-gather.4.cloned.1.call-update
  12.4 0.0 all-gather.6.cloned.1.call-start
  12.4 797.8 %all-gather.4.cloned.1.call-done = bf16[8192,2560]{1,0:T(8,128)(2,1)} async-done(((bf16[1024,2560]{1,0:T(8,128)(2,1)}), bf16[8192,2560]{1,0:T(8,128)(2,1)}) %all-gather.4.cloned.1.call-update) | async-done | bytes 41943056 | tf_op jit(solution)/shard_map/all_gather | solution.py:107
  810.2 0.0 all-gather.6.cloned.1.call-update
  810.3 0.7 copy-done.10
  810.9 0.5 copy-done.7
  811.5 0.3 multiply_reduce_fusion
  811.8 0.1 rsqrt.21
  811.9 0.6 fusion.74
  812.6 0.6 iota_compare_fusion.2
  813.2 1.3 broadcast_add_fusion
  814.5 1.2 iota_compare_fusion.1
  815.7 0.1 add_convert_fusion.2
  815.8 4.9 fusion.9
  820.8 0.7 compare_and_fusion
  821.4 0.9 fusion.40
  822.4 0.9 multiply_cosine_fusion
  823.3 0.3 fusion.32
  823.6 12.1 %fusion.11 = bf16[384,8192]{1,0:T(8,128)(2,1)} fusion(bf16[1,384,8192]{2,1,0:T(8,128)(2,1)} %param.6, f32[8192]{0:T(1024)S(1)} %convert_element_type.70, f32[384]{0:T(512)S(1)} %add_rsqrt_fusion), kind=kLoop, calls=%fused_computation.16 | loop fusion | flops 12582912 | bytes 12617216 | tf_op jit(solution)/shard_map/convert_element_type | solution.py:23
  835.6 95.3 %all-gather.6.cloned.1.call-done = bf16[8192,5120]{1,0:T(8,128)(2,1)} async-done(((bf16[8192,2560]{1,0:T(8,128)(2,1)}), bf16[8192,5120]{1,0:T(8,128)(2,1)}) %all-gather.6.cloned.1.call-update) | async-done | bytes 83886096 | tf_op jit(solution)/shard_map/all_gather | solution.py:108
  931.0 47.5 %fusion.16 = f32[448,5120]{1,0:T(8,128)} fusion(bf16[8192,5120]{1,0:T(8,128)(2,1)} %all-gather.6.cloned.1.call-done, bf16[64,8192]{1,0:T(8,128)(2,1)S(1)} %fusion.32, bf16[384,8192]{1,0:T(8,128)(2,1)} %fusion.11, f32[5120]{0:T(1024)S(1)} %convert_element_type.76), kind=kOutput, calls=%fused_computation.24 | convolution fusion | flops 37597937664 | bytes 100421632 | tf_op jit(solution)/shard_map/dot_general | solution.py:109
  978.5 10.8 copy.20
  989.3 1.3 slice.92
  990.6 8.8 fusion.92
  999.4 3.1 copy.59
  1002.5 0.3 copy.55
  1002.8 0.4 add_convert_fusion.1
  1003.2 0.0 copy-start.3
  1003.2 0.7 copy-done.3
  1004.0 0.2 fusion.59
  1004.2 2.5 all_gather.15
  1006.7 6.5 copy.56
  1013.2 6.5 copy.57
  1019.7 6.3 add_convert_fusion
  1026.1 0.1 pad_maximum_fusion.1
  1026.3 1.6 copy-done.1
  1027.9 1.1 copy-done.2
  1029.0 1.9 fusion.25
  1030.9 2.7 collective-permute-start.1
  1033.6 26.4 %fusion.93 = (f32[4,8,384]{2,1,0:T(8,128)S(1)}, f32[4,8,384,768]{2,3,1,0:T(8,128)}) fusion(pred[384,768]{0,1:T(8,128)(4,1)} %fusion.40, bf16[768,4,128]{2,0,1:T(8,128)(2,1)} %all_gather.15, bf16[448,4,8,64]{3,0,2,1:T(8,128)(2,1)} %copy-done.2, bf16[448,4,8,64]{3,0,2,1:T(8,128)(2,1)} %copy-done.1), kind=kOutput, calls=%fused_computation.139 | convolution fusion | flops 4901044736 | bytes 54640640 | tf_op jit(solution)/shard_map/sub | solution.py:143
  1060.0 1.0 slice.91
  1061.1 2.5 all-gather
  1063.6 15.2 %fusion.30 = bf16[4,128,8,384]{3,1,2,0:T(8,128)(2,1)} fusion(f32[4,8,384,768]{2,3,1,0:T(8,128)} %get-tuple-element.19, f32[4,8,384]{2,1,0:T(8,128)S(1)} %get-tuple-element.18, bf16[768,4,1,128]{0,3,1,2:T(8,128)(2,1)} %all-gather), kind=kOutput, calls=%fused_computation.45 | convolution fusion | flops 2436366336 | bytes 41730048 | tf_op jit(solution)/shard_map/aprk,kaz->rapz/dot_general | solution.py:48
  1078.8 4.6 copy.34
  1083.5 1.8 select_reduce_fusion.1
  1085.2 0.3 collective-permute-start
  1085.6 0.8 fusion.28
  1086.4 1.4 fusion.57
  1087.8 2.1 fusion.33
  1089.9 0.0 copy-start.8
  1089.9 1.3 fusion.41
  1091.2 0.1 copy.29
  1091.3 0.1 stack.9
  1091.4 1.8 fusion.22
  1093.2 0.1 fusion.58
  1093.4 0.8 fusion.29
  1094.2 1.3 fusion.64
  1095.5 27.3 %collective-permute-done = bf16[768,4,128]{0,2,1:T(8,128)(2,1)} collective-permute-done((bf16[768,4,128]{0,2,1:T(8,128)(2,1)}, bf16[768,4,128]{0,2,1:T(8,128)(2,1)}, u32[]{:S(2)}, u32[]{:S(2)}) %collective-permute-start) | collective-permute-done | bytes 786464 | tf_op jit(solution)/shard_map/ppermute | solution.py:17
  1122.9 2.2 fusion.42
  1125.0 0.1 copy.33
  1125.1 0.1 stack.10
  1125.3 0.8 pad_maximum_fusion
  (33 shorter events, 0.1 us)
Async XLA Ops:
  7.2 803.1 %all-gather.4.cloned.1.call-start = ((), (), s32[]{:S(2)}) async-start(), calls=%async_computation | async-start | bytes 47185920 | tf_op jit(solution)/shard_map/all_gather | solution.py:107
  12.4 918.6 %all-gather.6.cloned.1.call-start = ((), (), s32[]{:S(2)}) async-start(), calls=%async_computation.1 | async-start | bytes 125829120 | tf_op jit(solution)/shard_map/all_gather | solution.py:108
  810.2 0.7 copy-start.10
  810.2 1.2 copy-start.7
  810.2 1.6 copy-start.11
  810.2 1.7 copy-start.13
  990.6 8.8 copy-start
  1003.2 0.8 copy-start.3
  1003.2 1.0 copy-start.5
  1026.1 1.8 copy-start.1
  1026.1 2.9 copy-start.2
  1030.9 60.5 %collective-permute-start.1 = (bf16[768,4,128]{2,0,1:T(8,128)(2,1)}, bf16[768,4,128]{2,0,1:T(8,128)(2,1)}, u32[]{:S(2)}, u32[]{:S(2)}) collective-permute-start(bf16[768,4,128]{2,0,1:T(8,128)(2,1)} %all_gather.15), channel_id=1, source_target_pairs={{16,0},{20,4},{24,8},{28,12},{0,16},{4,20},{8,24},{12,28},{17,1},{... | collective-permute-start | bytes 2359304 | tf_op jit(solution)/shard_map/ppermute | solution.py:17
  1078.8 4.6 copy-start.9
  1083.5 2.9 copy-start.4
  1083.5 2.9 copy-start.6
  1085.2 37.6 %collective-permute-start = (bf16[768,4,128]{0,2,1:T(8,128)(2,1)}, bf16[768,4,128]{0,2,1:T(8,128)(2,1)}, u32[]{:S(2)}, u32[]{:S(2)}) collective-permute-start(bf16[768,4,128]{0,2,1:T(8,128)(2,1)} %bitcast.4), channel_id=1, source_target_pairs={{16,0},{20,4},{24,8},{28,12},{0,16},{4,20},{8,24},{12,28},{17,1},{... | collective-permute-start | bytes 2359304 | tf_op jit(solution)/shard_map/ppermute | solution.py:17
  1087.8 3.6 copy-start.12
  1089.9 3.4 copy-start.8
Sparse Core Ops, SparseCore 0:
  12.5 797.6 all-gather.3
  811.8 119.1 all-gather.5
where the time goes:
time: 1130 us
  waiting for transfers between devices  921 us (82%)
  matrix products  103 us (9%)
  local copies, waits for them, and re-layouts  53.4 us (5%)
  other arithmetic  33.8 us (3%)
  between operations  14.4 us (1%)
    all_gather x1, waiting for transfers between devices, on_device(): columns = lax.all_gather(own_cols, 'grp', axis=0, tiled=True)  798 us
    all_gather x1, waiting for transfers between devices, on_device(): complete = lax.all_gather(columns, 'rep', axis=1, tiled=True)  95.3 us
    dot_general x1, matrix products, on_device(): projected = jnp.dot(normed, complete, preferred_element_type=jnp.float32)  47.5 us
    ppermute x2, waiting for transfers between devices, shifted(): return lax.ppermute(block, axis, route)  27.4 us
    sub x1, matrix products, on_device(): exponent = jnp.where(allowed, jnp.exp(scores - highest), 0.0)  26.4 us
    unnamed x32, local copies, waits for them, and re-layouts  22.7 us
  transfers between devices with their start and end apart: 4, of which 3 were waited for; matrix products, arithmetic and copies ran while one was open for 7% of the time, Pallas kernels for 0%

commit v1 on v0

--- a/solution.py
+++ b/solution.py
@@ -105,7 +105,9 @@
     share_cols = qkv_weight.shape[1] // rep_count
     own_cols = lax.dynamic_slice_in_dim(qkv_weight, rep_here * share_cols, share_cols, 1)
     columns = lax.all_gather(own_cols, "grp", axis=0, tiled=True)
-    complete = lax.all_gather(columns, "rep", axis=1, tiled=True)
+    complete = jnp.concatenate(
+        lax.all_to_all(jnp.stack([columns] * lax.axis_size("rep")), "rep", 0, 0), axis=1
+    )
     projected = jnp.dot(normed, complete, preferred_element_type=jnp.float32)
     projected = (projected + qkv_bias.astype(jnp.float32)).reshape(
         normed.shape[0], heads_here, QPK + 2, HD

time: 1130 us -> 1220 us (1.080)
  blocking collectives: 5 us -> 142 us
  waiting for transfers between devices: 921 us -> 806 us
  other arithmetic: 33.8 us -> 82.6 us
    all_to_all x0 -> x1, blocking collectives: none -> 137 us  [on_device(): lax.all_to_all(jnp.stack([columns] * lax.axis_size('rep')), 'rep', 0, 0)]
    all_gather x1 -> x0, waiting for transfers between devices: 95.3 us -> none  [on_device(): complete = lax.all_gather(columns, 'rep', axis=1, tiled=True)]
    another operation x2 -> x3, other arithmetic: 6.72 us -> 62 us  [the longest x1 55.3 us: on_device(): jnp.stack([columns] * lax.axis_size('rep'))]
    all_gather x1, waiting for transfers between devices: 798 us -> 779 us  [on_device(): columns = lax.all_gather(own_cols, 'grp', axis=0, tiled=True)]
    unnamed x32 -> x47, local copies, waits for them, and re-layouts: 22.7 us -> 30.6 us
  transfers between devices with their start and end apart: 4 -> 3, of which waited for: 3 -> 2; matrix products, arithmetic and copies ran while one was open for 7% -> 6% of each run, Pallas kernels for 0% -> 0%
where the time goes in v1:
time: 1220 us; the launch traced here: 1210 us
  waiting for transfers between devices  806 us (66%)
  blocking collectives  142 us (12%)
  matrix products  104 us (9%)
  other arithmetic  82.6 us (7%)
  local copies, waits for them, and re-layouts  61.3 us (5%)
  between operations  14.4 us (1%)
    all_gather x1, waiting for transfers between devices, on_device(): columns = lax.all_gather(own_cols, 'grp', axis=0, tiled=True)  779 us
    all_to_all x1, blocking collectives, on_device(): lax.all_to_all(jnp.stack([columns] * lax.axis_size('rep')), 'rep', 0, 0)  137 us
    another operation x1, other arithmetic, on_device(): jnp.stack([columns] * lax.axis_size('rep'))  55.3 us
    dot_general x1, matrix products, on_device(): projected = jnp.dot(normed, complete, preferred_element_type=jnp.float32)  48.5 us
    unnamed x47, local copies, waits for them, and re-layouts  30.6 us
    ppermute x2, waiting for transfers between devices, shifted(): return lax.ppermute(block, axis, route)  27.1 us
    sub x1, matrix products, on_device(): exponent = jnp.where(allowed, jnp.exp(scores - highest), 0.0)  26.4 us
  transfers between devices with their start and end apart: 3, of which 2 were waited for; matrix products, arithmetic and copies ran while one was open for 6% of the time, Pallas kernels for 0%

profile of v1, /device:TPU:0, one launch (start us, length us, event | category | flops | bytes accessed | tf_op | source)
XLA Modules:
  0.0 1213.3 jit_solution(17081389708292132550)
XLA Ops:
  7.2 0.0 all-gather.3.cloned.1.call-start
  7.2 5.1 constant_dynamic-slice_fusion
  12.4 8.0 copy.56
  20.3 0.0 slice-start
  20.3 0.0 all-gather.3.cloned.1.call-update
  20.4 0.7 copy-done.13
  21.0 0.5 copy-done.7
  21.6 0.3 multiply_reduce_fusion
  21.9 0.1 rsqrt.21
  22.0 0.6 fusion.74
  22.6 0.6 iota_compare_fusion.2
  23.3 1.3 broadcast_add_fusion
  24.6 1.2 iota_compare_fusion.1
  25.8 0.1 add_convert_fusion.2
  25.9 4.3 fusion.9
  30.2 0.7 compare_and_fusion
  30.9 1.0 fusion.40
  31.8 1.7 multiply_cosine_fusion
  33.5 1.3 fusion.32
  34.8 4.5 fusion.11
  39.3 778.9 %all-gather.3.cloned.1.call-done = bf16[8192,2560]{0,1:T(8,128)(2,1)} async-done(((bf16[1024,2560]{0,1:T(8,128)(2,1)}), bf16[8192,2560]{0,1:T(8,128)(2,1)}) %all-gather.3.cloned.1.call-update) | async-done | bytes 41943056 | tf_op jit(solution)/shard_map/all_gather | solution.py:107
  818.2 55.3 %pad_maximum_fusion = bf16[2,8192,2560]{1,2,0:T(8,128)(2,1)} fusion(bf16[1,8192,2560]{1,2,0:T(8,128)(2,1)} %bitcast.157), kind=kLoop, calls=%fused_computation.1 | loop fusion | flops 41943040 | bytes 125829120 | tf_op jit(solution)/shard_map/stack | solution.py:109
  873.5 0.0 copy-start.11
  873.5 136.7 %all_to_all.5 = bf16[2,8192,2560]{1,2,0:T(8,128)(2,1)} all-to-all(bf16[2,8192,2560]{1,2,0:T(8,128)(2,1)} %pad_maximum_fusion), channel_id=1, replica_groups=mesh['grp'=8,'rep'=2,'tp'=2] {'rep'}, dimensions={0} | all-to-all | bytes 167772160 | tf_op jit(solution)/shard_map/all_to_all | solution.py:109
  1010.2 48.5 %fusion.16 = f32[448,5120]{1,0:T(8,128)} fusion(bf16[8192,5120]{0,1:T(8,128)(2,1)} %bitcast.5, bf16[64,8192]{1,0:T(8,128)(2,1)S(1)} %copy-done.11, bf16[384,8192]{1,0:T(8,128)(2,1)} %fusion.11, f32[5120]{0:T(1024)S(1)} %convert_element_type.76), kind=kOutput, calls=%fused_computation.25 | convolution fusion | flops 37597937664 | bytes 100421632 | tf_op jit(solution)/shard_map/dot_general | solution.py:111
  1058.7 10.8 copy.21
  1069.5 1.3 slice.92
  1070.8 8.8 fusion.92
  1079.6 3.1 copy.61
  1082.7 0.3 copy.57
  1083.0 0.4 add_convert_fusion.1
  1083.5 0.7 copy-done.3
  1084.2 0.2 fusion.59
  1084.4 2.7 all_gather.11
  1087.2 6.5 copy.58
  1093.7 6.5 copy.59
  1100.2 6.3 add_convert_fusion
  1106.6 0.1 pad_maximum_fusion.2
  1106.7 1.6 copy-done.1
  1108.3 1.1 copy-done.2
  1109.4 1.9 fusion.25
  1111.3 2.4 collective-permute-start.1
  1113.7 26.4 %fusion.93 = (f32[4,8,384]{2,1,0:T(8,128)S(1)}, f32[4,8,384,768]{2,3,1,0:T(8,128)}) fusion(pred[384,768]{0,1:T(8,128)(4,1)} %fusion.40, bf16[768,4,128]{2,0,1:T(8,128)(2,1)} %all_gather.11, bf16[448,4,8,64]{3,0,2,1:T(8,128)(2,1)} %copy-done.2, bf16[448,4,8,64]{3,0,2,1:T(8,128)(2,1)} %copy-done.1), kind=kOutput, calls=%fused_computation.140 | convolution fusion | flops 4901044736 | bytes 54640640 | tf_op jit(solution)/shard_map/sub | solution.py:145
  1140.1 1.0 slice.91
  1141.2 2.8 all-gather
  1143.9 15.1 %fusion.30 = bf16[4,128,8,384]{3,1,2,0:T(8,128)(2,1)} fusion(f32[4,8,384,768]{2,3,1,0:T(8,128)} %get-tuple-element.19, f32[4,8,384]{2,1,0:T(8,128)S(1)} %get-tuple-element.18, bf16[768,4,1,128]{0,3,1,2:T(8,128)(2,1)} %all-gather), kind=kOutput, calls=%fused_computation.46 | convolution fusion | flops 2436366336 | bytes 41730048 | tf_op jit(solution)/shard_map/aprk,kaz->rapz/dot_general | solution.py:48
  1159.1 4.6 copy.35
  1163.7 1.8 select_reduce_fusion.1
  1165.5 0.6 collective-permute-start
  1166.1 0.8 fusion.28
  1167.0 1.4 fusion.57
  1168.3 2.1 fusion.33
  1170.4 1.3 fusion.41
  1171.7 0.1 copy.30
  1171.8 0.1 stack.18
  1172.0 1.8 fusion.22
  1173.8 0.1 fusion.58
  1173.9 0.8 fusion.29
  1174.8 1.3 fusion.64
  1176.1 27.1 %collective-permute-done = bf16[768,4,128]{0,2,1:T(8,128)(2,1)} collective-permute-done((bf16[768,4,128]{0,2,1:T(8,128)(2,1)}, bf16[768,4,128]{0,2,1:T(8,128)(2,1)}, u32[]{:S(2)}, u32[]{:S(2)}) %collective-permute-start) | collective-permute-done | bytes 786464 | tf_op jit(solution)/shard_map/ppermute | solution.py:17
  1203.2 2.2 fusion.42
  1205.4 0.1 copy.34
  1205.5 0.1 stack.19
  1205.6 0.8 pad_maximum_fusion.1
  (48 shorter events, 0.1 us)
Async XLA Ops:
  7.2 811.0 %all-gather.3.cloned.1.call-start = ((), (), s32[]{:S(2)}) async-start(), calls=%async_computation.1 | async-start | bytes 47185920 | tf_op jit(solution)/shard_map/all_gather | solution.py:107
  20.3 0.7 copy-start.13
  20.3 1.2 copy-start.7
  20.3 1.6 copy-start.14
  20.3 1.7 copy-start.18
  20.3 14.4 %slice-start = ((s8[6291456]{0:T(1024)(128)(4,1)}), s8[2097152]{0:T(1024)(128)(4,1)S(1)}, s32[]{:S(2)}) async-start(s8[6291456]{0:T(1024)(128)(4,1)} %bitcast.158), calls=%async_computation.2 | async-start | bytes 4194304
  23.3 8.5 copy-start.15
  25.9 8.8 slice-start.1
  873.5 136.7 %copy-start.11 = (bf16[64,8192]{1,0:T(8,128)(2,1)S(1)}, bf16[64,8192]{1,0:T(8,128)(2,1)}, u32[]{:S(2)}) copy-start(bf16[64,8192]{1,0:T(8,128)(2,1)} %fusion.32) | copy-start | bytes 3145732
  1070.8 8.8 copy-start
  1079.6 3.4 copy-start.9
  1079.6 3.5 copy-start.10
  1083.4 0.8 copy-start.3
  1083.4 1.0 copy-start.5
  1106.5 1.8 copy-start.1
  1106.5 2.9 copy-start.2
  1106.6 2.9 copy-start.16
  1111.3 60.7 %collective-permute-start.1 = (bf16[768,4,128]{2,0,1:T(8,128)(2,1)}, bf16[768,4,128]{2,0,1:T(8,128)(2,1)}, u32[]{:S(2)}, u32[]{:S(2)}) collective-permute-start(bf16[768,4,128]{2,0,1:T(8,128)(2,1)} %all_gather.11), channel_id=1, source_target_pairs={{16,0},{20,4},{24,8},{28,12},{0,16},{4,20},{8,24},{12,28},{17,1},{... | collective-permute-start | bytes 2359304 | tf_op jit(solution)/shard_map/ppermute | solution.py:17
  1159.1 4.6 copy-start.12
  1163.7 3.2 copy-start.4
  1163.7 3.3 copy-start.6
  1165.5 37.7 %collective-permute-start = (bf16[768,4,128]{0,2,1:T(8,128)(2,1)}, bf16[768,4,128]{0,2,1:T(8,128)(2,1)}, u32[]{:S(2)}, u32[]{:S(2)}) collective-permute-start(bf16[768,4,128]{0,2,1:T(8,128)(2,1)} %bitcast.7), channel_id=1, source_target_pairs={{16,0},{20,4},{24,8},{28,12},{0,16},{4,20},{8,24},{12,28},{17,1},{... | collective-permute-start | bytes 2359304 | tf_op jit(solution)/shard_map/ppermute | solution.py:17
  1168.3 3.6 copy-start.17
  1170.4 3.4 copy-start.8
Sparse Core Ops, SparseCore 0:
  20.5 797.6 all-gather.2
